TPU v7x, 512 devices: a whole 4x8x8 slice. The times are simulated.
512 devices in a mesh: req: 64 (over x, y, core), tp: 8 (over z).
Axes of the slice: x: 4, y: 8, z: 8, core: 2. Of those that a mesh axis runs over, the one named last changes fastest.
Arguments:
- patches: bfloat16 [114688, 1664], P('req', 'tp'), may hold values from -48 to 48
- ln_gain: bfloat16 [1664], P('tp'), may hold values from 0.099609375 to 1.8984375
- ln_bias: bfloat16 [1664], P('tp'), may hold values from -3 to 3
- merge_weight: bfloat16 [4, 1664, 1664], P(None, 'tp'), may hold values from -0.078125 to 0.078125
- text_rows: bfloat16 [32768, 1664], P('req', 'tp'), may hold values from -48 to 48
- norm_gain: bfloat16 [1664], replicated, may hold values from 0.099609375 to 1.8984375
- qkv_weight: bfloat16 [1664, 4992], P('req', 'tp'), may hold values from -0.15625 to 0.15625
- token_pos: int32 [28672], P('req'), may hold values from 0 to 32767, as said below
- text_len: int32 [8], replicated, may hold values from 1 to 4096, as said below
Outputs:
- qkv_rows: bfloat16 [32768, 4992], P('req', 'tp')
Inputs may be any that keep to these rules, and one draw needn't show every extreme that they name: `token_pos`: all distinct. A device's merged tokens form 32 images of consecutive rows, each a multiple of 2 and at most 16 tokens, each written to consecutive positions that one device holds; a device's images go to 32 different devices and every device receives exactly 32 images. In every draw some image has 16 tokens. `text_len`: every image position of a request lies below its length.
All inputs are finite; a program needn't handle non-finite values.
Results may differ from a plain program's by a relative error of at most 0.0063.
Values may be sent and summed in bfloat16 or wider, within the bound.
A program may use at most 128 MiB of HBM per device.

v0:
```python
import jax
import jax.numpy as jnp
from jax import lax
from jax.sharding import PartitionSpec as P

DV = 1664
SEQ = 4096


EPSILON = 1e-06


def shards(
    patches, ln_gain, ln_bias, merge_weight, text_rows, norm_gain, qkv_weight, token_pos, text_len
):
    values = patches.astype(jnp.float32)
    sum_part = jnp.sum(values, axis=1)
    square_part = jnp.sum(values * values, axis=1)
    sum_total, square_total = lax.psum((sum_part, square_part), "tp")
    row_mean = (sum_total / DV)[:, None]
    second = (square_total / DV)[:, None]
    normed = (
        (values - row_mean)
        * lax.rsqrt(second - row_mean * row_mean + EPSILON)
        * ln_gain.astype(jnp.float32)
        + ln_bias.astype(jnp.float32)
    ).astype(jnp.bfloat16)
    width_part = patches.shape[1]
    grouped = normed.reshape(patches.shape[0] // 4, 4, width_part)
    partial_value = jnp.einsum(
        "mkf,kfd->md", grouped, merge_weight, preferred_element_type=jnp.float32
    )
    merged = lax.psum_scatter(partial_value, "tp", scatter_dimension=1, tiled=True).astype(
        jnp.bfloat16
    )
    row_count = text_rows.shape[0]
    base_row = lax.axis_index("req") * row_count
    piece_rows = lax.all_gather(merged, "req", axis=0, tiled=True)
    piece_pos = lax.all_gather(token_pos, "req", axis=0, tiled=True)
    local_pos = piece_pos - base_row
    inside = (local_pos >= 0) & (local_pos < row_count)
    combined = text_rows.at[jnp.where(inside, local_pos, row_count)].set(piece_rows, mode="drop")
    full_rows = lax.all_gather(combined, "tp", axis=1, tiled=True).astype(jnp.float32)
    scaled = (
        full_rows
        * lax.rsqrt(jnp.mean(full_rows * full_rows, axis=1, keepdims=True) + EPSILON)
        * norm_gain.astype(jnp.float32)
    ).astype(jnp.bfloat16)
    whole_weight = lax.all_gather(qkv_weight, "req", axis=0, tiled=True)
    projected = jnp.dot(scaled, whole_weight, preferred_element_type=jnp.float32)
    position = base_row + jnp.arange(row_count, dtype=jnp.int32)
    request = position // SEQ
    request_ids = jnp.arange(text_len.shape[0], dtype=jnp.int32)
    limits = jnp.sum(
        jnp.where(request[:, None] == request_ids[None, :], text_len[None, :], 0), axis=1
    )
    keep_row = position % SEQ < limits
    return jnp.where(keep_row[:, None], projected, 0.0).astype(jnp.bfloat16)


def solution(mesh):
    placed = (
        P("req", "tp"),
        P("tp"),
        P("tp"),
        P(None, "tp", None),
        P("req", "tp"),
        P(),
        P("req", "tp"),
        P("req"),
        P(),
    )
    return jax.shard_map(
        shards, mesh=mesh, in_specs=placed, out_specs=P("req", "tp"), check_vma=False
    )
```

profile of v0, /device:TPU:1, one launch (start us, length us, event | category | flops | bytes accessed | tf_op | source)
XLA Modules:
  0.0 532.0 jit_solution(7624971386064106252)
XLA Ops:
  7.4 1.5 convert_reduce_fusion
  8.9 0.7 convert_element_type.28
  9.5 0.7 convert_element_type.29
  10.2 29.8 %all-reduce.1 = (f32[1792]{0:T(1024)S(1)}, f32[1792]{0:T(1024)S(1)}) all-reduce(f32[1792]{0:T(1024)S(1)} %get-tuple-element.6, f32[1792]{0:T(1024)S(1)} %get-tuple-element.5), channel_id=1, replica_groups=mesh['req'=64,'tp'=8] {'tp'}, use_global_device_ids=true, to_apply=%region_4.0 | all-reduce | flops 3584 | bytes 28672 | tf_op jit(solution)/shard_map/psum | solution.py:19
  40.0 1.4 fusion.10
  41.4 1.3 copy.22
  42.7 2.5 reshape.56
  45.2 4.9 convolution_bitcast_fusion
  50.2 1.3 dynamic-slice
  52.2 0.3 dynamic-update-slice
  52.5 0.6 copy-done.1
  53.2 52.2 %reduce-scatter.2.cloned.1.call-done = f32[448,208]{0,1:T(8,128)} async-done(((f32[448,1664]{0,1:T(8,128)}), f32[448,208]{0,1:T(8,128)}) %reduce-scatter.2.cloned.1.call-update) | async-done | bytes 372752 | tf_op jit(solution)/shard_map/reduce_scatter | solution.py:33
  105.4 1.7 convert_bitcast_fusion
  107.2 0.5 all-gather.10.cloned.1.call-update
  108.0 133.9 %all-reduce.4.cloned.1.call-done = s32[28672]{0:T(1024)} async-done(((s32[28672]{0:T(1024)}), s32[28672]{0:T(1024)}) %all-reduce.4.cloned.1.call-update) | async-done | bytes 114704
  241.8 0.9 compare_select_fusion
  242.8 97.6 %all-gather.8.cloned.1.call-done = bf16[64,448,208]{1,2,0:T(8,128)(2,1)} async-done(((bf16[1,448,208]{1,2,0:T(8,128)(2,1)}), bf16[64,448,208]{1,2,0:T(8,128)(2,1)}) %all-gather.8.cloned.1.call-update) | async-done | bytes 11927568 | tf_op jit(solution)/shard_map/all_gather | solution.py:38
  340.3 19.8 %copy.28 = bf16[64,448,208]{2,1,0:T(8,128)(2,1)} copy(bf16[64,448,208]{1,2,0:T(8,128)(2,1)} %all-gather.8.cloned.1.call-done) | data formatting | bytes 23855104
  360.1 120.4 %scatter_fusion = bf16[512,208]{1,0:T(8,128)(2,1)S(1)} fusion(bf16[512,208]{1,0:T(8,128)(2,1)S(1)} %copy.25, s32[28672]{0:T(1024)S(1)} %compare_select_fusion, bf16[28672,208]{1,0:T(8,128)(2,1)} %bitcast.9), kind=kCustom, calls=%fused_computation | custom fusion | bytes 35897344 | tf_op jit(solution)/shard_map/scatter | solution.py:42
  480.5 0.8 copy.27
  481.5 4.3 reshape.72
  485.8 32.2 %all-gather.6.cloned.1.call-done = bf16[512,1664]{0,1:T(8,128)(2,1)} async-done(((bf16[512,208]{0,1:T(8,128)(2,1)}), bf16[512,1664]{0,1:T(8,128)(2,1)}) %all-gather.6.cloned.1.call-update) | async-done | bytes 1703952 | tf_op jit(solution)/shard_map/all_gather | solution.py:43
  518.0 1.9 fusion
  519.8 4.5 fusion.15
  (29 shorter events, 0.6 us)
Async XLA Ops:
  7.4 37.8 %copy-start = (bf16[4,208,1664]{2,1,0:T(8,128)(2,1)S(1)}, bf16[4,208,1664]{2,1,0:T(8,128)(2,1)}, u32[]{:S(2)}) copy-start(bf16[4,208,1664]{2,1,0:T(8,128)(2,1)} %param.12) | copy-start | bytes 8306692
  7.4 98.1 %reduce-scatter.2.cloned.1.call-start = ((), (), s32[]{:S(2)}) async-start(), calls=%async_computation.1 | async-start | bytes 3833856 | tf_op jit(solution)/shard_map/reduce_scatter | solution.py:33
  50.1 2.1 copy-start.4
  50.1 57.7 %copy-start.2 = (bf16[512,208]{0,1:T(8,128)(2,1)S(1)}, bf16[512,208]{0,1:T(8,128)(2,1)}, u32[]{:S(2)}) copy-start(bf16[512,208]{0,1:T(8,128)(2,1)} %param.13) | copy-start | bytes 638980
  50.2 191.7 %all-reduce.4.cloned.1.call-start = ((), (), s32[]{:S(2)}) async-start(), calls=%async_computation.3 | async-start | bytes 229376
  52.5 0.6 copy-start.1
  53.2 287.2 %all-gather.8.cloned.1.call-start = ((), (), s32[]{:S(2)}) async-start(), calls=%async_computation.4 | async-start | bytes 13844480 | tf_op jit(solution)/shard_map/all_gather | solution.py:38
  107.2 374.3 %all-gather.10.cloned.1.call-start = ((), (), s32[]{:S(2)}) async-start(), calls=%async_computation.5 | async-start | bytes 2662400 | tf_op jit(solution)/shard_map/all_gather | solution.py:49
  107.7 410.2 %all-gather.6.cloned.1.call-start = ((), (), s32[]{:S(2)}) async-start(), calls=%async_computation.2 | async-start | bytes 1916928 | tf_op jit(solution)/shard_map/all_gather | solution.py:43
  360.1 121.2 %copy-start.3 = (bf16[1664]{0:T(1024)(128)(2,1)S(1)}, bf16[1664]{0:T(1024)(128)(2,1)}, u32[]{:S(2)}) copy-start(bf16[1664]{0:T(1024)(128)(2,1)} %param.14) | copy-start | bytes 9988
  360.1 121.3 %copy-start.5 = (s32[8]{0:T(128)S(1)}, s32[8]{0:T(128)}, u32[]{:S(2)}) copy-start(s32[8]{0:T(128)} %param.17) | copy-start | bytes 100
Sparse Core Ops, SparseCore 0:
  50.3 55.1 reduce-scatter.1
Sparse Core Ops, SparseCore 1:
  54.1 187.7 all-reduce.3
  245.0 95.2 all-gather.7
  343.5 80.8 all-gather.9
  481.4 36.5 all-gather.5
where the time goes:
time: 536 us; the launch traced here: 532 us
  waiting for transfers between devices  316 us (59%)
  local copies, waits for them, and re-layouts  151 us (28%)
  blocking collectives  29.8 us (6%)
  between operations  15.8 us (3%)
  matrix products  9.48 us (2%)
  other arithmetic  8.89 us (2%)
    unnamed x6, waiting for transfers between devices  134 us
    scatter x2, local copies, waits for them, and re-layouts, shards(): text_rows.at[jnp.where(inside, local_pos, row_count)]  121 us
    all_gather x1, waiting for transfers between devices, shards(): piece_rows = lax.all_gather(merged, 'req', axis=0, tiled=True)  97.6 us
    reduce_scatter x1, waiting for transfers between devices, shards(): lax.psum_scatter(partial_value, 'tp', scatter_dimension=1, tiled=True)  52.2 us
    all_gather x1, waiting for transfers between devices, shards(): lax.all_gather(combined, 'tp', axis=1, tiled=True).astype(jnp.float32)  32.2 us
    psum x1, blocking collectives, shards(): sum_total, square_total = lax.psum((sum_part, square_part), 'tp')  29.8 us
    unnamed x18, local copies, waits for them, and re-layouts  26.5 us
  transfers between devices with their start and end apart: 5, of which 4 were waited for; matrix products, arithmetic and copies ran while one was open for 28% of the time, Pallas kernels for 0%

commit v1 on v0

v1 whole, which is shorter than its diff:
```python
import functools

import jax
import jax.numpy as jnp
from jax import lax
from jax.experimental import pallas as pl
from jax.experimental.pallas import tpu as pltpu
from jax.sharding import PartitionSpec as P

EPSILON = 1e-06
SEQ = 4096
MESH = pl.DeviceIdType.MESH
SLOT = 16
F32 = jnp.float32
BF16 = jnp.bfloat16


def nt_dot(a, b):
    return lax.dot_general(a, b, (((1,), (1,)), ((), ())), preferred_element_type=F32)


def nn_dot(a, b):
    return lax.dot_general(a, b, (((1,), (0,)), ((), ())), preferred_element_type=F32)


def tn_dot(a, b):
    return lax.dot_general(a, b, (((0,), (0,)), ((), ())), preferred_element_type=F32)


def kernel(
    nx, ny, nc, nz,
    patches, ln_gain, ln_bias, merge_weight, text_rows, norm_gain, qkv_weight, token_pos, text_len,
    out,
    weight, values, stats, columns, partial_t, rs_send, rs_recv, merged, select, slots, landed, text_t,
    full, gathered, expanded, scaled_weight, total, gain_column, tokens,
    local_sem, stat_send, stat_recv, rs_send_sem, rs_recv_sem, slot_send, slot_recv,
    ag_send_sem, ag_recv_sem, wy_send, wy_recv, wx_send, wx_recv, wc_send, wc_recv,
):
    nr = nx * ny * nc
    rows, width = patches.shape
    windows = rows // 4
    text = text_rows.shape[0]
    model = nz * width
    depth = qkv_weight.shape[0]
    z = lax.axis_index("tp")
    c = lax.axis_index("req")
    core = lax.rem(c, nc)
    y = lax.rem(c // nc, ny)
    x = c // (nc * ny)

    def wrap(value):
        return lax.rem(value + nz, nz)

    def wait_bytes(ref, sem):
        pltpu.make_async_copy(ref, ref, sem).wait()

    fetch = pltpu.make_async_copy(merge_weight, weight, local_sem.at[0])
    fetch.start()

    barrier = pltpu.get_barrier_semaphore()

    @pl.loop(1, nz)
    def _(k):
        pl.semaphore_signal(barrier, inc=1, device_id=(c, lax.rem(z + k, nz)), device_id_type=MESH)

    @pl.loop(1, nr)
    def _(k):
        pl.semaphore_signal(barrier, inc=1, device_id=(lax.rem(c + k, nr), z), device_id_type=MESH)

    raw = patches[...]
    wide = raw.astype(F32)
    square = wide * wide
    high = square.astype(BF16)
    low = (square - high.astype(F32)).astype(BF16)
    ones = jnp.ones((8, width), BF16)
    sums = nt_dot(ones, raw)
    squares = nt_dot(ones, high) + nt_dot(ones, low)
    stats[z, 0:1, :] = sums[0:1, :]
    stats[z, 1:2, :] = squares[0:1, :]
    for p in range(values.shape[0]):
        size = min(128, width - p * 128)
        values[p, :, 0:size] = wide[:, p * 128 : p * 128 + size]

    pl.semaphore_wait(barrier, nz - 1 + nr - 1)

    @pl.loop(1, nz)
    def _(k):
        pltpu.make_async_remote_copy(
            stats.at[z], stats.at[z], stat_send, stat_recv,
            device_id=(c, lax.rem(z + k, nz)), device_id_type=MESH,
        ).start()

    own = pltpu.make_async_copy(qkv_weight, gathered.at[core, x, y], local_sem.at[1])
    own.start()

    @pl.loop(1, ny)
    def _(k):
        there = (x * ny + lax.rem(y + k, ny)) * nc + core
        pltpu.make_async_remote_copy(
            qkv_weight, gathered.at[core, x, y], wy_send, wy_recv,
            device_id=(there, z), device_id_type=MESH,
        ).start()

    tokens[...] = jnp.full(tokens.shape, -text, jnp.int32)
    tokens[0:1, 0:windows] = token_pos[...]
    place = tokens[...]
    receiver = place // text
    lane = lax.broadcasted_iota(jnp.int32, place.shape, 1)
    rank = jnp.zeros(place.shape, jnp.int32)
    for k in range(1, SLOT):
        before = pltpu.roll(receiver, k, 1)
        rank += jnp.where((before == receiver) & (lane >= k), 1, 0)
    slot = (receiver * SLOT + rank)[0:1, :]
    inner = lax.rem(place, text)[0:1, :]
    step_rows = select.shape[1]
    for q in range(select.shape[0]):
        wanted = lax.broadcasted_iota(jnp.int32, (step_rows, place.shape[1]), 0) + q * step_rows
        select[q] = jnp.where(wanted == slot, 1.0, 0.0).astype(BF16)
    merged[...] = jnp.zeros(merged.shape, BF16)
    info_rows = lax.broadcasted_iota(jnp.int32, (16, place.shape[1]), 0)
    info = jnp.where(
        info_rows == 0, lax.rem(inner, 16), jnp.where(info_rows == 1, inner // 16, jnp.where(info_rows == 2, 1, 0))
    )
    merged[width : width + 16, :] = info.astype(F32).astype(BF16)
    text_t[...] = text_rows[...].astype(F32).T
    gain_column[...] = jnp.broadcast_to(norm_gain[...].astype(F32), (8, model)).T

    wait_bytes(stats.at[pl.ds(0, nz - 1)], stat_recv)
    wait_bytes(stats.at[pl.ds(0, nz - 1)], stat_send)
    whole = stats[0]
    for k in range(1, nz):
        whole = whole + stats[k]
    whole = whole / model
    mean = whole[0:1, :]
    scale = lax.rsqrt(whole[1:2, :] - mean * mean + EPSILON)
    which = lax.broadcasted_iota(jnp.int32, (8, rows), 0)
    columns[:, 0:8] = jnp.where(which == 0, mean, scale).T
    gain = ln_gain[...].astype(F32)
    bias = ln_bias[...].astype(F32)
    parts = []
    for k in range(4):
        one = jnp.concatenate(
            [values[p, pl.ds(k, windows, stride=4), :] for p in range(values.shape[0])], axis=1
        )[:, 0:width]
        stat = columns[pl.ds(k, windows, stride=4), :]
        parts.append(((one - stat[:, 0:1]) * stat[:, 1:2] * gain + bias).astype(BF16))

    fetch.wait()
    start = 0
    while start < model:
        size = min(256, model - start)
        tile = None
        for k in range(4):
            term = nn_dot(parts[k], weight[k * width : (k + 1) * width, start : start + size])
            tile = term if tile is None else tile + term
        partial_t[start : start + size, :] = tile.T
        start += size

    half = (width // 2 + 15) // 16 * 16
    spans = ((0, half), (half, width - half))
    chains = []
    for d in (0, 1):
        for h in (0, 1):
            chains.append((d, h, nz // 2 if d == h else nz - 1 - nz // 2))

    def ring_copy(sem_pair, source, target, d):
        step = 1 if d == 0 else -1
        return pltpu.make_async_remote_copy(
            source, target, sem_pair[0], sem_pair[1], device_id=(c, wrap(z + step)), device_id_type=MESH
        )

    def rs_copy(d, h, t):
        size = spans[h][1]
        return ring_copy(
            (rs_send_sem.at[d, h, t], rs_recv_sem.at[d, h, t]),
            rs_send.at[d, h, t, pl.ds(0, size)],
            rs_recv.at[d, h, t, pl.ds(0, size)],
            d,
        )

    def rows_of(block, h):
        at, size = spans[h]
        return partial_t[pl.ds(pl.multiple_of(block * width + at, 8), size), :]

    steps = nz // 2
    for t in range(steps):
        for d, h, length in chains:
            if t >= length:
                continue
            size = spans[h][1]
            step = 1 if d == 0 else -1
            value = rows_of(wrap(z + step * (length - t)), h)
            if t > 0:
                rs_copy(d, h, t - 1).wait_recv()
                value = value + rs_recv[d, h, t - 1, 0:size, :].astype(F32)
            rs_send[d, h, t, 0:size, :] = value.astype(BF16)
            rs_copy(d, h, t).start()
        if t == 1:
            own.wait()
            wait_bytes(gathered.at[core, x, pl.ds(0, ny - 1)], wy_recv)
            wait_bytes(gathered.at[core, x, pl.ds(0, ny - 1)], wy_send)

            @pl.loop(1, nx)
            def _(k):
                there = (lax.rem(x + k, nx) * ny + y) * nc + core
                pltpu.make_async_remote_copy(
                    gathered.at[core, x], gathered.at[core, x], wx_send, wx_recv,
                    device_id=(there, z), device_id_type=MESH,
                ).start()

    for h in (0, 1):
        at, size = spans[h]
        value = rows_of(z, h)
        for d, hh, length in chains:
            if hh == h:
                rs_copy(d, h, length - 1).wait_recv()
                value = value + rs_recv[d, h, length - 1, 0:size, :].astype(F32)
        merged[at : at + size, 0:windows] = value.astype(BF16)
    for d, h, length in chains:
        for t in range(length):
            rs_copy(d, h, t).wait_send()

    per = step_rows // SLOT
    token_rows = merged[...]
    for q in range(select.shape[0]):
        block = nt_dot(select[q], token_rows).astype(BF16)
        slots[q * per : (q + 1) * per] = block.reshape(per, SLOT, block.shape[1])
    keep_own = pltpu.make_async_copy(slots.at[c], landed.at[c], local_sem.at[2])
    keep_own.start()

    @pl.loop(1, nr)
    def _(k):
        there = lax.rem(c + k, nr)
        pltpu.make_async_remote_copy(
            slots.at[there], landed.at[c], slot_send, slot_recv, device_id=(there, z), device_id_type=MESH
        ).start()

    wait_bytes(gathered.at[core, pl.ds(0, nx - 1)], wx_recv)
    wait_bytes(gathered.at[core, pl.ds(0, nx - 1)], wx_send)
    sibling = x * ny * nc + y * nc + (nc - 1 - core)
    swap = pltpu.make_async_remote_copy(
        gathered.at[core], gathered.at[core], wc_send, wc_recv, device_id=(sibling, z), device_id_type=MESH
    )
    swap.start()
    swap.wait()
    for ic in range(nc):
        for ix in range(nx):
            for iy in range(ny):
                row = ((ix * ny + iy) * nc + ic) * depth
                expanded[row : row + depth, :] = gathered[ic, ix, iy].astype(F32)
    for d in range(nz):
        at = d * width
        scaled_weight[d] = (expanded[at : at + width, :] * gain_column[at : at + width, 0:1]).astype(BF16)

    keep_own.wait()
    wait_bytes(landed.at[pl.ds(0, nr - 1)], slot_recv)
    wait_bytes(slots.at[pl.ds(0, nr - 1)], slot_send)
    arrived = landed[...].reshape(nr * SLOT, landed.shape[2])
    info = arrived[:, width : width + 8].astype(F32)
    position = info[:, 1:2] * 16.0 + info[:, 0:1] + (info[:, 2:3] - 1.0) * (4.0 * text)
    position = position.astype(jnp.int32)
    spread = jnp.where(
        position == lax.broadcasted_iota(jnp.int32, (nr * SLOT, text), 1), 1.0, 0.0
    ).astype(BF16)
    placed = tn_dot(arrived, spread)
    covered = placed[width + 2 : width + 3, :] > 0.5
    full[z] = jnp.where(covered, placed[0:width, :], text_t[...]).astype(BF16)

    def ag_copy(d, h, t):
        step = 1 if d == 0 else -1
        at, size = spans[h]
        block = full.at[wrap(z - step * t), pl.ds(at, size)]
        return ring_copy((ag_send_sem.at[d, h, t], ag_recv_sem.at[d, h, t]), block, block, d)

    for d, h, length in chains:
        ag_copy(d, h, 0).start()

    def project(block):
        piece = full[block]
        wide = piece.astype(F32)
        return tn_dot(piece, scaled_weight[block]), jnp.sum(wide * wide, axis=0, keepdims=True)

    product, norm = project(z)
    total[...] = product
    for t in range(steps):
        for d, h, length in chains:
            if t < length:
                ag_copy(d, h, t).wait_recv()
                if t + 1 < length:
                    ag_copy(d, h, t + 1).start()
        for block in (z + t + 1, z - t - 1) if t + 1 < nz - t - 1 else (z + t + 1,):
            product, part = project(wrap(lax.rem(block, nz)))
            total[...] += product
            norm = norm + part
    for d, h, length in chains:
        for t in range(length):
            ag_copy(d, h, t).wait_send()

    row_scale = lax.rsqrt(norm / model + EPSILON)
    row_scale = jnp.broadcast_to(row_scale, (8, text)).T[:, 0:1]
    per_request = SEQ // text
    limit = text_len[c // per_request]
    position = lax.broadcasted_iota(jnp.int32, (text, 1), 0) + lax.rem(c, per_request) * text
    out[...] = jnp.where(position < limit, total[...] * row_scale, 0.0).astype(BF16)


def solution(mesh, grid=None):
    nz = mesh.shape["tp"]
    nx, ny, nc = grid or (4, mesh.shape["req"] // 8, 2)

    def shards(
        patches, ln_gain, ln_bias, merge_weight, text_rows, norm_gain, qkv_weight, token_pos, text_len
    ):
        rows, width = patches.shape
        windows = rows // 4
        text = text_rows.shape[0]
        depth, heads = qkv_weight.shape
        model = nz * width
        nr = nx * ny * nc
        lanes = (windows + 127) // 128 * 128
        payload = (width + 16 + 127) // 128 * 128
        half = (width // 2 + 15) // 16 * 16
        steps = nz // 2
        chunk = min(256, nr * SLOT)
        dma = pltpu.SemaphoreType.DMA
        vmem = pl.BlockSpec(memory_space=pltpu.VMEM)
        return pl.pallas_call(
            functools.partial(kernel, nx, ny, nc, nz),
            out_shape=jax.ShapeDtypeStruct((text, heads), BF16),
            in_specs=[
                vmem, vmem, vmem, pl.BlockSpec(memory_space=pl.ANY), vmem, vmem, vmem, vmem,
                pl.BlockSpec(memory_space=pltpu.SMEM),
            ],
            out_specs=vmem,
            scratch_shapes=[
                pltpu.VMEM((4 * width, model), BF16),
                pltpu.VMEM(((width + 127) // 128, rows, 128), F32),
                pltpu.VMEM((nz, 2, rows), F32),
                pltpu.VMEM((rows, 128), F32),
                pltpu.VMEM((model, windows), F32),
                pltpu.VMEM((2, 2, steps, half, windows), BF16),
                pltpu.VMEM((2, 2, steps, half, windows), BF16),
                pltpu.VMEM((payload, lanes), BF16),
                pltpu.VMEM((nr * SLOT // chunk, chunk, lanes), BF16),
                pltpu.VMEM((nr, SLOT, payload), BF16),
                pltpu.VMEM((nr, SLOT, payload), BF16),
                pltpu.VMEM((width, text), F32),
                pltpu.VMEM((nz, width, text), BF16),
                pltpu.VMEM((nc, nx, ny, depth, heads), BF16),
                pltpu.VMEM((model, heads), F32),
                pltpu.VMEM((nz, width, heads), BF16),
                pltpu.VMEM((text, heads), F32),
                pltpu.VMEM((model, 8), F32),
                pltpu.VMEM((8, lanes), jnp.int32),
                dma((3,)), dma, dma, dma((2, 2, steps)), dma((2, 2, steps)), dma, dma,
                dma((2, 2, steps)), dma((2, 2, steps)), dma, dma, dma, dma, dma, dma,
            ],
            compiler_params=pltpu.CompilerParams(
                collective_id=0, has_side_effects=True, vmem_limit_bytes=56 << 20
            ),
        )(
            patches,
            ln_gain.reshape(1, width),
            ln_bias.reshape(1, width),
            merge_weight.reshape(4 * width, model),
            text_rows,
            norm_gain.reshape(1, model),
            qkv_weight,
            token_pos.reshape(1, windows),
            text_len,
        )

    placed = (
        P("req", "tp"),
        P("tp"),
        P("tp"),
        P(None, "tp", None),
        P("req", "tp"),
        P(),
        P("req", "tp"),
        P("req"),
        P(),
    )
    return jax.shard_map(
        shards, mesh=mesh, in_specs=placed, out_specs=P("req", "tp"), check_vma=False
    )
```

time: 536 us -> 93.1 us (0.17)
  waiting for transfers between devices: 316 us -> 0 us
  local copies, waits for them, and re-layouts: 151 us -> 9.86 us
  Pallas kernels: 0 us -> 81.8 us
  blocking collectives: 29.8 us -> 0 us
  between operations: 15.8 us -> 0.01 us
  matrix products: 9.48 us -> 0 us
  other arithmetic: 8.89 us -> 0 us
    unnamed x6 -> x0, waiting for transfers between devices: 134 us -> none
    all_gather x3 -> x0, waiting for transfers between devices: 130 us -> none  [the longest x1 97.6 us: shards(): piece_rows = lax.all_gather(merged, 'req', axis=0, tiled=True)]
    scatter x2 -> x0, local copies, waits for them, and re-layouts: 121 us -> none  [shards(): text_rows.at[jnp.where(inside, local_pos, row_count)]]
    pallas_call x0 -> x1, Pallas kernels: none -> 81.8 us  [shards(): pl.pallas_call(functools.partial(kernel, nx, ny, nc, nz), out_shape=jax.S...]
    reduce_scatter x1 -> x0, waiting for transfers between devices: 52.2 us -> none  [shards(): lax.psum_scatter(partial_value, 'tp', scatter_dimension=1, tiled=True)]
    psum x1 -> x0, blocking collectives: 29.8 us -> none  [shards(): sum_total, square_total = lax.psum((sum_part, square_part), 'tp')]
    unnamed x18 -> x2, local copies, waits for them, and re-layouts: 26.5 us -> 3.97 us
    dot_general x2 -> x0, matrix products: 9.48 us -> none  [the longest x1 4.94 us: shards(): jnp.einsum('mkf,kfd->md', grouped, merge_weight, preferred_element_type=j...]
  transfers between devices with their start and end apart: 5 -> 0, of which waited for: 4 -> 0; matrix products, arithmetic and copies ran while one was open for 28% -> 0% of each run, Pallas kernels for 0% -> 0%
where the time goes in v1:
time: 93.1 us; the launch traced here: 91.7 us
  Pallas kernels  81.8 us (88%)
  local copies, waits for them, and re-layouts  9.86 us (11%)
    pallas_call x1, Pallas kernels, shards(): pl.pallas_call(functools.partial(kernel, nx, ny, nc, nz), out_shape=jax.S...  81.8 us
    unnamed x2, local copies, waits for them, and re-layouts  3.97 us
    pallas_call x1, local copies, waits for them, and re-layouts, shards(): pl.pallas_call(functools.partial(kernel, nx, ny, nc, nz), out_shape=jax.S...  2.16 us

profile of v1, /device:TPU:1, one launch (start us, length us, event | category | flops | bytes accessed | tf_op | source)
XLA Modules:
  0.0 91.7 jit_solution(275047501477972241)
XLA Ops:
  0.0 1.2 %reshape.15.ln_gain = bf16[1,208]{1,0:T(2,128)(2,1)} reshape(bf16[208]{0:T(256)(128)(2,1)} %param.10) | data formatting | bytes 832 | tf_op jit(solution)/shard_map/reshape | solution.py:363
  1.2 1.2 %reshape.16.ln_bias = bf16[1,208]{1,0:T(2,128)(2,1)} reshape(bf16[208]{0:T(256)(128)(2,1)} %param.11) | data formatting | bytes 832 | tf_op jit(solution)/shard_map/reshape | solution.py:364
  2.5 1.3 %reshape.18.norm_gain = bf16[1,1664]{1,0:T(2,128)(2,1)} reshape(bf16[1664]{0:T(1024)(128)(2,1)} %param.14) | data formatting | bytes 6656 | tf_op jit(solution)/shard_map/reshape | solution.py:367
  3.7 1.8 %copy.11.text_rows = bf16[512,208]{1,0:T(8,128)(2,1)} copy(bf16[512,208]{0,1:T(8,128)(2,1)} %param.13) | data formatting | bytes 425984 | tf_op args[4]
  5.5 2.2 %copy.10.patches = bf16[1792,208]{1,0:T(8,128)(2,1)} copy(bf16[1792,208]{0,1:T(8,128)(2,1)} %param.9) | data formatting | bytes 1490944 | tf_op args[0]
  7.7 81.8 %shard_map.91 = bf16[512,624]{1,0:T(8,128)(2,1)} custom-call(bf16[1792,208]{1,0:T(8,128)(2,1)} %copy.10.patches, bf16[1,208]{1,0:T(2,128)(2,1)} %reshape.15.ln_gain, bf16[1,208]{1,0:T(2,128)(2,1)} %reshape.16.ln_bias, bf16[832,1664]{1,0:T(8,128)(2,1)} %bitcast.2, bf16[512,208]{1,0:T(8,128)(2,1)} %copy.11.text_rows, bf16[1,1664]{1,0:T(2,128)(2,1)} %reshape.18.norm_gain, ...), custom_call_target="tpu_custom_call" | custom-call | tf_op jit(solution)/shard_map/pallas_call | solution.py:327
  89.6 2.2 %copy.12 = bf16[512,624]{0,1:T(8,128)(2,1)} copy(bf16[512,624]{1,0:T(8,128)(2,1)} %shard_map.91) | data formatting | bytes 1277952 | tf_op jit(solution)/shard_map/pallas_call | solution.py:327

commit v2 on v1

v2 whole, which is shorter than its diff:
```python
import functools

import jax
import jax.numpy as jnp
from jax import lax
from jax.experimental import pallas as pl
from jax.experimental.pallas import tpu as pltpu
from jax.sharding import PartitionSpec as P

EPSILON = 1e-06
SEQ = 4096
MESH = pl.DeviceIdType.MESH
SLOT = 16
F32 = jnp.float32
BF16 = jnp.bfloat16


def nt_dot(a, b):
    return lax.dot_general(a, b, (((1,), (1,)), ((), ())), preferred_element_type=F32)


def nn_dot(a, b):
    return lax.dot_general(a, b, (((1,), (0,)), ((), ())), preferred_element_type=F32)


def tn_dot(a, b):
    return lax.dot_general(a, b, (((0,), (0,)), ((), ())), preferred_element_type=F32)


def halves(start, size):
    first = (size // 2 + 15) // 16 * 16
    return [(start, first), (start + first, size - first)]


def kernel(
    nx, ny, nc, nz,
    patches_hbm, gain_hbm, bias_hbm, merge_hbm, text_hbm, norm_hbm, qkv_hbm, token_pos, text_len,
    out_t,
    patches_t, ln_gain, ln_bias, weight, text_t, norm_gain,
    values, stats, columns, partial_t, rs_send, rs_recv, merged, select, slots, landed, spread,
    full, gathered, expanded, total, gain_column, tokens,
    local_sem, stat_send, stat_recv, rs_send_sem, rs_recv_sem, slot_send, slot_recv,
    ag_send_sem, ag_recv_sem, wy_send, wy_recv, wx_send, wx_recv, wc_send, wc_recv,
):
    nr = nx * ny * nc
    width, rows = patches_t.shape
    windows = rows // 4
    text = text_t.shape[1]
    model = nz * width
    depth = qkv_hbm.shape[0]
    z = lax.axis_index("tp")
    c = lax.axis_index("req")
    core = lax.rem(c, nc)
    y = lax.rem(c // nc, ny)
    x = c // (nc * ny)

    first_chunk = (width // 2 + 15) // 16 * 16
    chunks = ((0, first_chunk), (first_chunk, width - first_chunk))
    pieces = halves(*chunks[0]) + halves(*chunks[1])
    steps = nz // 2
    whole_tiles, rest = windows // 128, windows % 128
    assert rest == 64

    def reach(d, s):
        return steps if (d == 0) == (s in (0, 3)) else nz - 1 - steps

    def wrap(value):
        return lax.rem(value + nz, nz)

    def wait_bytes(ref, sem):
        pltpu.make_async_copy(ref, ref, sem).wait()

    barrier = pltpu.get_barrier_semaphore()

    @pl.loop(1, nz)
    def _(k):
        pl.semaphore_signal(barrier, inc=1, device_id=(c, lax.rem(z + k, nz)), device_id_type=MESH)

    fetches = [
        pltpu.make_async_copy(source, target, local_sem.at[i])
        for i, (source, target) in enumerate((
            (patches_hbm, patches_t), (gain_hbm, ln_gain), (bias_hbm, ln_bias), (merge_hbm, weight),
            (text_hbm, text_t), (norm_hbm, norm_gain), (qkv_hbm, gathered.at[core, x, y]),
        ))
    ]
    for fetch in fetches:
        fetch.start()

    @pl.loop(1, nr)
    def _(k):
        pl.semaphore_signal(barrier, inc=1, device_id=(lax.rem(c + k, nr), z), device_id_type=MESH)

    fetches[0].wait()
    wide = patches_t[...].astype(F32)
    stats[z, 0:1, :] = jnp.sum(wide, axis=0, keepdims=True)
    stats[z, 1:2, :] = jnp.sum(wide * wide, axis=0, keepdims=True)
    pl.semaphore_wait(barrier, nz - 1 + nr - 1)

    @pl.loop(1, nz)
    def _(k):
        pltpu.make_async_remote_copy(
            stats.at[z], stats.at[z], stat_send, stat_recv,
            device_id=(c, lax.rem(z + k, nz)), device_id_type=MESH,
        ).start()

    fetches[6].wait()

    @pl.loop(1, ny)
    def _(k):
        there = (x * ny + lax.rem(y + k, ny)) * nc + core
        pltpu.make_async_remote_copy(
            gathered.at[core, x, y], gathered.at[core, x, y], wy_send, wy_recv,
            device_id=(there, z), device_id_type=MESH,
        ).start()

    for p in range(values.shape[0]):
        size = min(128, width - p * 128)
        values[p, :, 0:size] = patches_t[p * 128 : p * 128 + size, :].astype(F32).T

    tokens[...] = jnp.full(tokens.shape, -text, jnp.int32)
    tokens[0:1, 0:windows] = token_pos[...]
    place = tokens[...]
    receiver = place // text
    lane = lax.broadcasted_iota(jnp.int32, place.shape, 1)
    rank = jnp.zeros(place.shape, jnp.int32)
    for k in range(1, SLOT):
        before = pltpu.roll(receiver, k, 1)
        rank += jnp.where((before == receiver) & (lane >= k), 1, 0)
    slot = (receiver * SLOT + rank)[0:1, :]
    inner = lax.rem(place, text)[0:1, :]
    step_rows = select.shape[1]
    for q in range(select.shape[0]):
        wanted = lax.broadcasted_iota(jnp.int32, (step_rows, place.shape[1]), 0) + q * step_rows
        select[q] = jnp.where(wanted == slot, 1.0, 0.0).astype(BF16)
    merged[...] = jnp.zeros(merged.shape, BF16)
    info_rows = lax.broadcasted_iota(jnp.int32, (16, place.shape[1]), 0)
    info = jnp.where(
        info_rows == 0, lax.rem(inner, 16), jnp.where(info_rows == 1, inner // 16, jnp.where(info_rows == 2, 1, 0))
    )
    merged[0, first_chunk : first_chunk + 16, :] = info.astype(F32).astype(BF16)
    fetches[1].wait()
    fetches[2].wait()
    fetches[4].wait()
    fetches[5].wait()
    gain_column[...] = jnp.broadcast_to(norm_gain[...].astype(F32).reshape(1, model), (8, model)).T
    gain = ln_gain[...].astype(F32).reshape(1, width)
    bias = ln_bias[...].astype(F32).reshape(1, width)
    fetches[3].wait()

    wait_bytes(stats.at[pl.ds(0, nz - 1)], stat_recv)
    wait_bytes(stats.at[pl.ds(0, nz - 1)], stat_send)
    whole = stats[0]
    for k in range(1, nz):
        whole = whole + stats[k]
    whole = whole / model
    mean = whole[0:1, :]
    scale = lax.rsqrt(whole[1:2, :] - mean * mean + EPSILON)
    which = lax.broadcasted_iota(jnp.int32, (8, rows), 0)
    columns[:, 0:8] = jnp.where(which == 0, mean, scale).T
    parts = []
    for k in range(4):
        one = jnp.concatenate(
            [values[p, pl.ds(k, windows, stride=4), :] for p in range(values.shape[0])], axis=1
        )[:, 0:width]
        stat = columns[pl.ds(k, windows, stride=4), :]
        parts.append(((one - stat[:, 0:1]) * stat[:, 1:2] * gain + bias).astype(BF16))

    start = 0
    while start < model:
        size = min(256, model - start)
        tile = None
        for k in range(4):
            term = nn_dot(parts[k], weight[k * width : (k + 1) * width, start : start + size])
            tile = term if tile is None else tile + term
        tile = tile.T
        for q in range(whole_tiles):
            partial_t[q, start : start + size, :] = tile[:, q * 128 : (q + 1) * 128]
        partial_t[whole_tiles, start : start + size, 0:rest] = tile[:, whole_tiles * 128 : windows]
        start += size

    wait_bytes(gathered.at[core, x, pl.ds(0, ny - 1)], wy_recv)
    wait_bytes(gathered.at[core, x, pl.ds(0, ny - 1)], wy_send)

    @pl.loop(1, nx)
    def _(k):
        there = (lax.rem(x + k, nx) * ny + y) * nc + core
        pltpu.make_async_remote_copy(
            gathered.at[core, x], gathered.at[core, x], wx_send, wx_recv,
            device_id=(there, z), device_id_type=MESH,
        ).start()

    def ring_copy(send, recv, source, target, d):
        step = 1 if d == 0 else -1
        return pltpu.make_async_remote_copy(
            source, target, send, recv, device_id=(c, wrap(z + step)), device_id_type=MESH
        )

    def packed_rows(s):
        size = pieces[s][1]
        return whole_tiles * size + size // 2

    def rs_copy(d, s, t):
        span = pl.ds(0, packed_rows(s))
        return ring_copy(
            rs_send_sem.at[d, s, t], rs_recv_sem.at[d, s, t],
            rs_send.at[d, s, t, span], rs_recv.at[d, s, t, span], d,
        )

    def own_rows(block, s):
        at, size = pieces[s]

        def load(tile, begin, count, lanes):
            return partial_t[tile, pl.ds(pl.multiple_of(block * width + begin, 8), count), 0:lanes]

        tiles = [load(q, at, size, 128) for q in range(whole_tiles)]
        low = load(whole_tiles, at, size // 2, rest)
        high = load(whole_tiles, at + size // 2, size // 2, rest)
        return jnp.concatenate(tiles + [jnp.concatenate([low, high], axis=1)], axis=0)

    order = [(s, d) for s in range(4) for d in (0, 1)]
    for t in range(steps):
        for s, d in order:
            if t >= reach(d, s):
                continue
            step = 1 if d == 0 else -1
            value = own_rows(wrap(z + step * (reach(d, s) - t)), s)
            if t > 0:
                rs_copy(d, s, t - 1).wait_recv()
                value = value + rs_recv[d, s, t - 1, 0 : packed_rows(s), :].astype(F32)
            rs_send[d, s, t, 0 : packed_rows(s), :] = value.astype(BF16)
            rs_copy(d, s, t).start()

    per = step_rows // SLOT

    def slot_copy(chunk, there):
        return pltpu.make_async_remote_copy(
            slots.at[chunk, there], landed.at[chunk, c], slot_send.at[chunk], slot_recv.at[chunk],
            device_id=(there, z), device_id_type=MESH,
        )

    for chunk in (0, 1):
        for s in (2 * chunk, 2 * chunk + 1):
            at, size = pieces[s]
            at -= chunks[chunk][0]
            value = own_rows(z, s)
            for d in (0, 1):
                rs_copy(d, s, reach(d, s) - 1).wait_recv()
                value = value + rs_recv[d, s, reach(d, s) - 1, 0 : packed_rows(s), :].astype(F32)
            for q in range(whole_tiles):
                merged[chunk, at : at + size, q * 128 : (q + 1) * 128] = value[q * size : (q + 1) * size].astype(BF16)
            for p in (0, 1):
                fold = value[whole_tiles * size :, p * rest : (p + 1) * rest]
                into = at + p * (size // 2)
                merged[chunk, into : into + size // 2, whole_tiles * 128 : windows] = fold.astype(BF16)
        token_rows = merged[chunk]
        for q in range(select.shape[0]):
            block = nt_dot(select[q], token_rows).astype(BF16)
            slots[chunk, q * per : (q + 1) * per] = block.reshape(per, SLOT, block.shape[1])
        keep_own = pltpu.make_async_copy(slots.at[chunk, c], landed.at[chunk, c], local_sem.at[7 + chunk])
        keep_own.start()

        @pl.loop(1, nr)
        def _(k):
            slot_copy(chunk, lax.rem(c + k, nr)).start()

    wait_bytes(gathered.at[core, pl.ds(0, nx - 1)], wx_recv)
    wait_bytes(gathered.at[core, pl.ds(0, nx - 1)], wx_send)
    sibling = x * ny * nc + y * nc + (nc - 1 - core)
    swap = pltpu.make_async_remote_copy(
        gathered.at[core], gathered.at[core], wc_send, wc_recv, device_id=(sibling, z), device_id_type=MESH
    )
    swap.start()
    for s, d in order:
        for t in range(reach(d, s)):
            rs_copy(d, s, t).wait_send()

    def ag_copy(d, s, t):
        step = 1 if d == 0 else -1
        at, size = pieces[s]
        block = full.at[wrap(z - step * t), pl.ds(at, size)]
        return ring_copy(ag_send_sem.at[d, s, t], ag_recv_sem.at[d, s, t], block, block, d)

    covered = None
    for chunk in (0, 1):
        at, size = chunks[chunk]
        pltpu.make_async_copy(slots.at[chunk, c], landed.at[chunk, c], local_sem.at[7 + chunk]).wait()
        wait_bytes(landed.at[chunk, pl.ds(0, nr - 1)], slot_recv.at[chunk])
        arrived = landed[chunk].reshape(nr * SLOT, landed.shape[3])
        if chunk == 0:
            info = arrived[:, size : size + 8].astype(F32)
            position = info[:, 1:2] * 16.0 + info[:, 0:1] + (info[:, 2:3] - 1.0) * (4.0 * text)
            position = position.astype(jnp.int32)
            spread[...] = jnp.where(
                position == lax.broadcasted_iota(jnp.int32, (nr * SLOT, text), 1), 1.0, 0.0
            ).astype(BF16)
        placed = tn_dot(arrived, spread[...])
        if chunk == 0:
            covered = placed[size + 2 : size + 3, :] > 0.5
        full[z, at : at + size, :] = jnp.where(
            covered, placed[0:size, :], text_t[at : at + size, :].astype(F32)
        ).astype(BF16)
        for s in (2 * chunk, 2 * chunk + 1):
            for d in (0, 1):
                ag_copy(d, s, 0).start()
    for chunk in (0, 1):
        wait_bytes(slots.at[chunk, pl.ds(0, nr - 1)], slot_send.at[chunk])
    swap.wait()

    group = width // depth

    def ready(block, i):
        for j in range(group):
            index = block * group + j
            expanded[i, j * depth : (j + 1) * depth, :] = gathered[
                lax.rem(index, nc), index // (nc * ny), lax.rem(index // nc, ny)
            ].astype(F32)
        gains = gain_column[pl.ds(pl.multiple_of(block * width, 8), width), :]
        return (expanded[i] * gains[:, 0:1]).astype(BF16)

    def project(block, block_weight):
        piece = full[block]
        wide = piece.astype(F32)
        return tn_dot(block_weight, piece), jnp.sum(wide * wide, axis=0, keepdims=True)

    product, norm = project(z, ready(z, 0))
    total[...] = product
    for t in range(steps):
        blocks = (z + t + 1, z - t - 1) if t + 1 < nz - t - 1 else (z + t + 1,)
        blocks = [wrap(lax.rem(block, nz)) for block in blocks]
        block_weights = [ready(block, i) for i, block in enumerate(blocks)]
        for s, d in order:
            if t < reach(d, s):
                ag_copy(d, s, t).wait_recv()
                if t + 1 < reach(d, s):
                    ag_copy(d, s, t + 1).start()
        for block, block_weight in zip(blocks, block_weights):
            product, part = project(block, block_weight)
            total[...] += product
            norm = norm + part

    row_scale = lax.rsqrt(norm / model + EPSILON)
    per_request = SEQ // text
    limit = text_len[c // per_request]
    position = lax.broadcasted_iota(jnp.int32, (1, text), 1) + lax.rem(c, per_request) * text
    out_t[...] = jnp.where(position < limit, total[...] * row_scale, 0.0).astype(BF16)
    for s, d in order:
        for t in range(reach(d, s)):
            ag_copy(d, s, t).wait_send()


def solution(mesh, grid=None):
    nz = mesh.shape["tp"]
    nx, ny, nc = grid or (4, mesh.shape["req"] // 8, 2)

    def shards(
        patches, ln_gain, ln_bias, merge_weight, text_rows, norm_gain, qkv_weight, token_pos, text_len
    ):
        rows, width = patches.shape
        windows = rows // 4
        text = text_rows.shape[0]
        depth, heads = qkv_weight.shape
        model = nz * width
        nr = nx * ny * nc
        lanes = (windows + 127) // 128 * 128
        first_chunk = (width // 2 + 15) // 16 * 16
        piece = halves(0, first_chunk)[0][1]
        packed = windows // 128 * piece + piece // 2
        steps = nz // 2
        chunk = min(256, nr * SLOT)
        dma = pltpu.SemaphoreType.DMA
        vmem = pl.BlockSpec(memory_space=pltpu.VMEM)
        hbm = pl.BlockSpec(memory_space=pl.ANY)
        ring = dma((2, 4, steps))
        return pl.pallas_call(
            functools.partial(kernel, nx, ny, nc, nz),
            out_shape=jax.ShapeDtypeStruct((heads, text), BF16),
            in_specs=[hbm] * 7 + [vmem, pl.BlockSpec(memory_space=pltpu.SMEM)],
            out_specs=vmem,
            scratch_shapes=[
                pltpu.VMEM((width, rows), BF16),
                pltpu.VMEM((width,), BF16),
                pltpu.VMEM((width,), BF16),
                pltpu.VMEM((4 * width, model), BF16),
                pltpu.VMEM((width, text), BF16),
                pltpu.VMEM((model,), BF16),
                pltpu.VMEM(((width + 127) // 128, rows, 128), F32),
                pltpu.VMEM((nz, 2, rows), F32),
                pltpu.VMEM((rows, 128), F32),
                pltpu.VMEM((windows // 128 + 1, model, 128), F32),
                pltpu.VMEM((2, 4, steps, packed, 128), BF16),
                pltpu.VMEM((2, 4, steps, packed, 128), BF16),
                pltpu.VMEM((2, 128, lanes), BF16),
                pltpu.VMEM((nr * SLOT // chunk, chunk, lanes), BF16),
                pltpu.VMEM((2, nr, SLOT, 128), BF16),
                pltpu.VMEM((2, nr, SLOT, 128), BF16),
                pltpu.VMEM((nr * SLOT, text), BF16),
                pltpu.VMEM((nz, width, text), BF16),
                pltpu.VMEM((nc, nx, ny, depth, heads), BF16),
                pltpu.VMEM((2, width, heads), F32),
                pltpu.VMEM((heads, text), F32),
                pltpu.VMEM((model, 8), F32),
                pltpu.VMEM((8, lanes), jnp.int32),
                dma((9,)), dma, dma, ring, ring, dma((2,)), dma((2,)), ring, ring,
                dma, dma, dma, dma, dma, dma,
            ],
            compiler_params=pltpu.CompilerParams(
                collective_id=0, has_side_effects=True, vmem_limit_bytes=56 << 20
            ),
        )(
            patches.T,
            ln_gain,
            ln_bias,
            merge_weight.reshape(4 * width, model),
            text_rows.T,
            norm_gain,
            qkv_weight,
            token_pos.reshape(1, windows),
            text_len,
        ).T

    placed = (
        P("req", "tp"),
        P("tp"),
        P("tp"),
        P(None, "tp", None),
        P("req", "tp"),
        P(),
        P("req", "tp"),
        P("req"),
        P(),
    )
    return jax.shard_map(
        shards, mesh=mesh, in_specs=placed, out_specs=P("req", "tp"), check_vma=False
    )
```

time: 93.1 us -> 78.2 us (0.84)
  local copies, waits for them, and re-layouts: 9.86 us -> 1.95 us
  Pallas kernels: 81.8 us -> 75 us
    pallas_call x1, Pallas kernels: 81.8 us -> 75 us  [shards(): pl.pallas_call(functools.partial(kernel, nx, ny, nc, nz), out_shape=jax.S...]
    reshape x3 -> x0, local copies, waits for them, and re-layouts: 3.74 us -> none  [the longest x1 1.28 us: shards(): norm_gain.reshape(1, model)]
    pallas_call x1 -> x0, local copies, waits for them, and re-layouts: 2.16 us -> none  [shards(): pl.pallas_call(functools.partial(kernel, nx, ny, nc, nz), out_shape=jax.S...]
    unnamed x2 -> x1, local copies, waits for them, and re-layouts: 3.97 us -> 1.95 us
where the time goes in v2:
time: 78.2 us; the launch traced here: 77 us
  Pallas kernels  75 us (96%)
  local copies, waits for them, and re-layouts  1.95 us (2%)
    pallas_call x1, Pallas kernels, shards(): pl.pallas_call(functools.partial(kernel, nx, ny, nc, nz), out_shape=jax.S...  75 us
    unnamed x1, local copies, waits for them, and re-layouts  1.95 us

profile of v2, /device:TPU:1, one launch (start us, length us, event | category | flops | bytes accessed | tf_op | source)
XLA Modules:
  0.0 77.0 jit_solution(8860022681465075024)
XLA Ops:
  0.0 75.0 %shard_map.91 = bf16[624,512]{1,0:T(8,128)(2,1)} custom-call(bf16[208,1792]{1,0:T(8,128)(2,1)} %bitcast.7, bf16[208]{0:T(256)(128)(2,1)} %gain_hbm.1, bf16[208]{0:T(256)(128)(2,1)} %bias_hbm.1, bf16[832,1664]{1,0:T(8,128)(2,1)} %bitcast.5, bf16[208,512]{1,0:T(8,128)(2,1)} %bitcast.8, bf16[1664]{0:T(1024)(128)(2,1)} %norm_hbm.1, bf16[26,624]{1,0:T(8,128)(2,1)} %qkv_hbm.1, ...), custom_call_target="tpu_custom_call" | custom-call | tf_op jit(solution)/shard_map/pallas_call | solution.py:374
  75.1 2.0 %copy.11 = bf16[512,624]{0,1:T(8,128)(2,1)} copy(bf16[512,624]{0,1:T(8,128)(2,1)} %bitcast.6) | data formatting | bytes 1277952

commit v3 on v2

--- a/solution.py
+++ b/solution.py
@@ -11,6 +11,7 @@
 SEQ = 4096
 MESH = pl.DeviceIdType.MESH
 SLOT = 16
+GROUPS = ((0,), (1,), (2,), (3,))
 F32 = jnp.float32
 BF16 = jnp.bfloat16
 
@@ -165,70 +166,74 @@
         stat = columns[pl.ds(k, windows, stride=4), :]
         parts.append(((one - stat[:, 0:1]) * stat[:, 1:2] * gain + bias).astype(BF16))
 
-    start = 0
-    while start < model:
-        size = min(256, model - start)
-        tile = None
-        for k in range(4):
-            term = nn_dot(parts[k], weight[k * width : (k + 1) * width, start : start + size])
-            tile = term if tile is None else tile + term
-        tile = tile.T
-        for q in range(whole_tiles):
-            partial_t[q, start : start + size, :] = tile[:, q * 128 : (q + 1) * 128]
-        partial_t[whole_tiles, start : start + size, 0:rest] = tile[:, whole_tiles * 128 : windows]
-        start += size
-
-    wait_bytes(gathered.at[core, x, pl.ds(0, ny - 1)], wy_recv)
-    wait_bytes(gathered.at[core, x, pl.ds(0, ny - 1)], wy_send)
-
-    @pl.loop(1, nx)
-    def _(k):
-        there = (lax.rem(x + k, nx) * ny + y) * nc + core
-        pltpu.make_async_remote_copy(
-            gathered.at[core, x], gathered.at[core, x], wx_send, wx_recv,
-            device_id=(there, z), device_id_type=MESH,
-        ).start()
-
     def ring_copy(send, recv, source, target, d):
         step = 1 if d == 0 else -1
         return pltpu.make_async_remote_copy(
             source, target, send, recv, device_id=(c, wrap(z + step)), device_id_type=MESH
         )
 
-    def packed_rows(s):
-        size = pieces[s][1]
-        return whole_tiles * size + size // 2
+    def piece_rows(s):
+        return width if s < whole_tiles else width // 2
 
     def rs_copy(d, s, t):
-        span = pl.ds(0, packed_rows(s))
+        span = pl.ds(0, piece_rows(s))
         return ring_copy(
             rs_send_sem.at[d, s, t], rs_recv_sem.at[d, s, t],
             rs_send.at[d, s, t, span], rs_recv.at[d, s, t, span], d,
         )
 
     def own_rows(block, s):
-        at, size = pieces[s]
-
-        def load(tile, begin, count, lanes):
-            return partial_t[tile, pl.ds(pl.multiple_of(block * width + begin, 8), count), 0:lanes]
-
-        tiles = [load(q, at, size, 128) for q in range(whole_tiles)]
-        low = load(whole_tiles, at, size // 2, rest)
-        high = load(whole_tiles, at + size // 2, size // 2, rest)
-        return jnp.concatenate(tiles + [jnp.concatenate([low, high], axis=1)], axis=0)
+        at = pl.multiple_of(block * width, 8)
+        if s < whole_tiles:
+            return partial_t[s, pl.ds(at, width), :]
+        low = partial_t[s, pl.ds(at, width // 2), 0:rest]
+        high = partial_t[s, pl.ds(at + width // 2, width // 2), 0:rest]
+        return jnp.concatenate([low, high], axis=1)
+
+    def rs_step(d, s, t):
+        step = 1 if d == 0 else -1
+        value = own_rows(wrap(z + step * (reach(d, s) - t)), s)
+        if t > 0:
+            rs_copy(d, s, t - 1).wait_recv()
+            value = value + rs_recv[d, s, t - 1, 0 : piece_rows(s), :].astype(F32)
+        rs_send[d, s, t, 0 : piece_rows(s), :] = value.astype(BF16)
+        rs_copy(d, s, t).start()
+
+    def x_stage():
+        wait_bytes(gathered.at[core, x, pl.ds(0, ny - 1)], wy_recv)
+        wait_bytes(gathered.at[core, x, pl.ds(0, ny - 1)], wy_send)
+
+        @pl.loop(1, nx)
+        def _(k):
+            there = (lax.rem(x + k, nx) * ny + y) * nc + core
+            pltpu.make_async_remote_copy(
+                gathered.at[core, x], gathered.at[core, x], wx_send, wx_recv,
+                device_id=(there, z), device_id_type=MESH,
+            ).start()
 
     order = [(s, d) for s in range(4) for d in (0, 1)]
-    for t in range(steps):
+    for group in GROUPS:
+        first, last = group[0] * 128, min((group[-1] + 1) * 128, windows)
+        start = 0
+        while start < model:
+            size = min(256, model - start)
+            tile = None
+            for k in range(4):
+                term = nn_dot(parts[k][first:last], weight[k * width : (k + 1) * width, start : start + size])
+                tile = term if tile is None else tile + term
+            tile = tile.T
+            for s in group:
+                at, lanes = s * 128 - first, min(128, windows - s * 128)
+                partial_t[s, start : start + size, 0:lanes] = tile[:, at : at + lanes]
+            start += size
+        for s in group:
+            for d in (0, 1):
+                rs_step(d, s, 0)
+    x_stage()
+    for t in range(1, steps):
         for s, d in order:
-            if t >= reach(d, s):
-                continue
-            step = 1 if d == 0 else -1
-            value = own_rows(wrap(z + step * (reach(d, s) - t)), s)
-            if t > 0:
-                rs_copy(d, s, t - 1).wait_recv()
-                value = value + rs_recv[d, s, t - 1, 0 : packed_rows(s), :].astype(F32)
-            rs_send[d, s, t, 0 : packed_rows(s), :] = value.astype(BF16)
-            rs_copy(d, s, t).start()
+            if t < reach(d, s):
+                rs_step(d, s, t)
 
     per = step_rows // SLOT
 
@@ -238,30 +243,32 @@
             device_id=(there, z), device_id_type=MESH,
         )
 
+    for s in range(4):
+        value = own_rows(z, s)
+        for d in (0, 1):
+            rs_copy(d, s, reach(d, s) - 1).wait_recv()
+            value = value + rs_recv[d, s, reach(d, s) - 1, 0 : piece_rows(s), :].astype(F32)
+        value = value.astype(BF16)
+        if s < whole_tiles:
+            merged[0, 0:first_chunk, s * 128 : (s + 1) * 128] = value[0:first_chunk]
+            merged[1, 0 : width - first_chunk, s * 128 : (s + 1) * 128] = value[first_chunk:]
+        else:
+            low, high, fold = value[:, 0:rest], value[:, rest : 2 * rest], width // 2
+            merged[0, 0:fold, s * 128 : windows] = low
+            merged[0, fold:first_chunk, s * 128 : windows] = high[0 : first_chunk - fold]
+            merged[1, 0 : width - first_chunk, s * 128 : windows] = high[first_chunk - fold :]
     for chunk in (0, 1):
-        for s in (2 * chunk, 2 * chunk + 1):
-            at, size = pieces[s]
-            at -= chunks[chunk][0]
-            value = own_rows(z, s)
-            for d in (0, 1):
-                rs_copy(d, s, reach(d, s) - 1).wait_recv()
-                value = value + rs_recv[d, s, reach(d, s) - 1, 0 : packed_rows(s), :].astype(F32)
-            for q in range(whole_tiles):
-                merged[chunk, at : at + size, q * 128 : (q + 1) * 128] = value[q * size : (q + 1) * size].astype(BF16)
-            for p in (0, 1):
-                fold = value[whole_tiles * size :, p * rest : (p + 1) * rest]
-                into = at + p * (size // 2)
-                merged[chunk, into : into + size // 2, whole_tiles * 128 : windows] = fold.astype(BF16)
         token_rows = merged[chunk]
-        for q in range(select.shape[0]):
-            block = nt_dot(select[q], token_rows).astype(BF16)
-            slots[chunk, q * per : (q + 1) * per] = block.reshape(per, SLOT, block.shape[1])
-        keep_own = pltpu.make_async_copy(slots.at[chunk, c], landed.at[chunk, c], local_sem.at[7 + chunk])
-        keep_own.start()
-
-        @pl.loop(1, nr)
-        def _(k):
-            slot_copy(chunk, lax.rem(c + k, nr)).start()
+        for q in range(nx):
+            there_x = lax.rem(x + q, nx)
+            block = nt_dot(select[there_x], token_rows).astype(BF16)
+            slots[chunk, pl.ds(there_x * per, per)] = block.reshape(per, SLOT, block.shape[1])
+            if q == 0:
+                pltpu.make_async_copy(slots.at[chunk, c], landed.at[chunk, c], local_sem.at[7 + chunk]).start()
+
+            @pl.loop(1 if q == 0 else 0, per)
+            def _(k):
+                slot_copy(chunk, there_x * per + lax.rem(y * nc + core + k, per)).start()
 
     wait_bytes(gathered.at[core, pl.ds(0, nx - 1)], wx_recv)
     wait_bytes(gathered.at[core, pl.ds(0, nx - 1)], wx_send)
@@ -363,17 +370,15 @@
         nr = nx * ny * nc
         lanes = (windows + 127) // 128 * 128
         first_chunk = (width // 2 + 15) // 16 * 16
-        piece = halves(0, first_chunk)[0][1]
-        packed = windows // 128 * piece + piece // 2
         steps = nz // 2
-        chunk = min(256, nr * SLOT)
+        chunk = ny * nc * SLOT
         dma = pltpu.SemaphoreType.DMA
         vmem = pl.BlockSpec(memory_space=pltpu.VMEM)
         hbm = pl.BlockSpec(memory_space=pl.ANY)
         ring = dma((2, 4, steps))
         return pl.pallas_call(
             functools.partial(kernel, nx, ny, nc, nz),
-            out_shape=jax.ShapeDtypeStruct((heads, text), BF16),
+            out_shape=pltpu.VMEM((heads, text), BF16),
             in_specs=[hbm] * 7 + [vmem, pl.BlockSpec(memory_space=pltpu.SMEM)],
             out_specs=vmem,
             scratch_shapes=[
@@ -387,10 +392,10 @@
                 pltpu.VMEM((nz, 2, rows), F32),
                 pltpu.VMEM((rows, 128), F32),
                 pltpu.VMEM((windows // 128 + 1, model, 128), F32),
-                pltpu.VMEM((2, 4, steps, packed, 128), BF16),
-                pltpu.VMEM((2, 4, steps, packed, 128), BF16),
+                pltpu.VMEM((2, 4, steps, width, 128), BF16),
+                pltpu.VMEM((2, 4, steps, width, 128), BF16),
                 pltpu.VMEM((2, 128, lanes), BF16),
-                pltpu.VMEM((nr * SLOT // chunk, chunk, lanes), BF16),
+                pltpu.VMEM((nx, chunk, lanes), BF16),
                 pltpu.VMEM((2, nr, SLOT, 128), BF16),
                 pltpu.VMEM((2, nr, SLOT, 128), BF16),
                 pltpu.VMEM((nr * SLOT, text), BF16),

time: 78.2 us -> 73.7 us (0.942); the launches traced: 77 us -> 73.5 us
  Pallas kernels: 75 us -> 72.7 us
  local copies, waits for them, and re-layouts: 1.95 us -> 0.83 us
    pallas_call x1, Pallas kernels: 75 us -> 72.7 us  [shards(): pl.pallas_call(functools.partial(kernel, nx, ny, nc, nz), out_shape=pltpu...]
    unnamed x1, local copies, waits for them, and re-layouts: 1.95 us -> 0.83 us
where the time goes in v3:
time: 73.7 us; the launch traced here: 73.5 us
  Pallas kernels  72.7 us (99%)
  local copies, waits for them, and re-layouts  0.83 us (1%)
    pallas_call x1, Pallas kernels, shards(): pl.pallas_call(functools.partial(kernel, nx, ny, nc, nz), out_shape=pltpu...  72.7 us

profile of v3, /device:TPU:1, one launch (start us, length us, event | category | flops | bytes accessed | tf_op | source)
XLA Modules:
  0.0 73.5 jit_solution(72503252551407551)
XLA Ops:
  0.0 72.7 %shard_map.91 = bf16[624,512]{1,0:T(8,128)(2,1)S(1)} custom-call(bf16[208,1792]{1,0:T(8,128)(2,1)} %bitcast.7, bf16[208]{0:T(256)(128)(2,1)} %gain_hbm.1, bf16[208]{0:T(256)(128)(2,1)} %bias_hbm.1, bf16[832,1664]{1,0:T(8,128)(2,1)} %bitcast.6, bf16[208,512]{1,0:T(8,128)(2,1)} %bitcast.8, bf16[1664]{0:T(1024)(128)(2,1)} %norm_hbm.1, bf16[26,624]{1,0:T(8,128)(2,1)} %qkv_hbm.1, ...), custom_call_target="tpu_custom_call" | custom-call | tf_op jit(solution)/shard_map/pallas_call | solution.py:379
  72.7 0.8 %copy.11 = bf16[512,624]{0,1:T(8,128)(2,1)} copy(bf16[512,624]{0,1:T(8,128)(2,1)S(1)} %bitcast.5) | data formatting | bytes 1277952

commit v4 on v3

--- a/solution.py
+++ b/solution.py
@@ -35,9 +35,9 @@
 
 def kernel(
     nx, ny, nc, nz,
-    patches_hbm, gain_hbm, bias_hbm, merge_hbm, text_hbm, norm_hbm, qkv_hbm, token_pos, text_len,
+    patches_hbm, gain_hbm, bias_hbm, merge_hbm, text_hbm, norm_hbm, qkv_hbm, token_hbm, length_hbm,
     out_t,
-    patches_t, ln_gain, ln_bias, weight, text_t, norm_gain,
+    token_pos, text_len, patches_t, ln_gain, ln_bias, weight, text_t, norm_gain,
     values, stats, columns, partial_t, rs_send, rs_recv, merged, select, slots, landed, spread,
     full, gathered, expanded, total, gain_column, tokens,
     local_sem, stat_send, stat_recv, rs_send_sem, rs_recv_sem, slot_send, slot_recv,
@@ -82,6 +82,7 @@
         for i, (source, target) in enumerate((
             (patches_hbm, patches_t), (gain_hbm, ln_gain), (bias_hbm, ln_bias), (merge_hbm, weight),
             (text_hbm, text_t), (norm_hbm, norm_gain), (qkv_hbm, gathered.at[core, x, y]),
+            (token_hbm, token_pos), (length_hbm, text_len),
         ))
     ]
     for fetch in fetches:
@@ -119,6 +120,7 @@
         values[p, :, 0:size] = patches_t[p * 128 : p * 128 + size, :].astype(F32).T
 
     tokens[...] = jnp.full(tokens.shape, -text, jnp.int32)
+    fetches[7].wait()
     tokens[0:1, 0:windows] = token_pos[...]
     place = tokens[...]
     receiver = place // text
@@ -143,6 +145,7 @@
     fetches[2].wait()
     fetches[4].wait()
     fetches[5].wait()
+    fetches[8].wait()
     gain_column[...] = jnp.broadcast_to(norm_gain[...].astype(F32).reshape(1, model), (8, model)).T
     gain = ln_gain[...].astype(F32).reshape(1, width)
     bias = ln_bias[...].astype(F32).reshape(1, width)
@@ -229,11 +232,12 @@
         for s in group:
             for d in (0, 1):
                 rs_step(d, s, 0)
-    x_stage()
     for t in range(1, steps):
         for s, d in order:
             if t < reach(d, s):
                 rs_step(d, s, t)
+        if t == 1:
+            x_stage()
 
     per = step_rows // SLOT
 
@@ -264,7 +268,7 @@
             block = nt_dot(select[there_x], token_rows).astype(BF16)
             slots[chunk, pl.ds(there_x * per, per)] = block.reshape(per, SLOT, block.shape[1])
             if q == 0:
-                pltpu.make_async_copy(slots.at[chunk, c], landed.at[chunk, c], local_sem.at[7 + chunk]).start()
+                pltpu.make_async_copy(slots.at[chunk, c], landed.at[chunk, c], local_sem.at[9 + chunk]).start()
 
             @pl.loop(1 if q == 0 else 0, per)
             def _(k):
@@ -290,7 +294,7 @@
     covered = None
     for chunk in (0, 1):
         at, size = chunks[chunk]
-        pltpu.make_async_copy(slots.at[chunk, c], landed.at[chunk, c], local_sem.at[7 + chunk]).wait()
+        pltpu.make_async_copy(slots.at[chunk, c], landed.at[chunk, c], local_sem.at[9 + chunk]).wait()
         wait_bytes(landed.at[chunk, pl.ds(0, nr - 1)], slot_recv.at[chunk])
         arrived = landed[chunk].reshape(nr * SLOT, landed.shape[3])
         if chunk == 0:
@@ -329,27 +333,33 @@
         wide = piece.astype(F32)
         return tn_dot(block_weight, piece), jnp.sum(wide * wide, axis=0, keepdims=True)
 
-    product, norm = project(z, ready(z, 0))
-    total[...] = product
+    def blocks_of(t):
+        both = (z + t + 1, z - t - 1) if t + 1 < nz - t - 1 else (z + t + 1,)
+        return [wrap(lax.rem(block, nz)) for block in both]
+
     for t in range(steps):
-        blocks = (z + t + 1, z - t - 1) if t + 1 < nz - t - 1 else (z + t + 1,)
-        blocks = [wrap(lax.rem(block, nz)) for block in blocks]
-        block_weights = [ready(block, i) for i, block in enumerate(blocks)]
         for s, d in order:
             if t < reach(d, s):
                 ag_copy(d, s, t).wait_recv()
                 if t + 1 < reach(d, s):
                     ag_copy(d, s, t + 1).start()
-        for block, block_weight in zip(blocks, block_weights):
+        if t == 0:
+            product, norm = project(z, ready(z, 2))
+            total[...] = product
+            block_weights = [ready(block, i) for i, block in enumerate(blocks_of(0))]
+        for block, block_weight in zip(blocks_of(t), block_weights):
             product, part = project(block, block_weight)
-            total[...] += product
             norm = norm + part
+            if t + 1 < steps:
+                total[...] += product
+        if t + 1 < steps:
+            block_weights = [ready(block, i) for i, block in enumerate(blocks_of(t + 1))]
 
     row_scale = lax.rsqrt(norm / model + EPSILON)
     per_request = SEQ // text
     limit = text_len[c // per_request]
     position = lax.broadcasted_iota(jnp.int32, (1, text), 1) + lax.rem(c, per_request) * text
-    out_t[...] = jnp.where(position < limit, total[...] * row_scale, 0.0).astype(BF16)
+    out_t[...] = jnp.where(position < limit, (total[...] + product) * row_scale, 0.0).astype(BF16)
     for s, d in order:
         for t in range(reach(d, s)):
             ag_copy(d, s, t).wait_send()
@@ -379,9 +389,11 @@
         return pl.pallas_call(
             functools.partial(kernel, nx, ny, nc, nz),
             out_shape=pltpu.VMEM((heads, text), BF16),
-            in_specs=[hbm] * 7 + [vmem, pl.BlockSpec(memory_space=pltpu.SMEM)],
+            in_specs=[hbm] * 9,
             out_specs=vmem,
             scratch_shapes=[
+                pltpu.VMEM((1, windows), jnp.int32),
+                pltpu.SMEM(text_len.shape, jnp.int32),
                 pltpu.VMEM((width, rows), BF16),
                 pltpu.VMEM((width,), BF16),
                 pltpu.VMEM((width,), BF16),
@@ -401,11 +413,11 @@
                 pltpu.VMEM((nr * SLOT, text), BF16),
                 pltpu.VMEM((nz, width, text), BF16),
                 pltpu.VMEM((nc, nx, ny, depth, heads), BF16),
-                pltpu.VMEM((2, width, heads), F32),
+                pltpu.VMEM((3, width, heads), F32),
                 pltpu.VMEM((heads, text), F32),
                 pltpu.VMEM((model, 8), F32),
                 pltpu.VMEM((8, lanes), jnp.int32),
-                dma((9,)), dma, dma, ring, ring, dma((2,)), dma((2,)), ring, ring,
+                dma((11,)), dma, dma, ring, ring, dma((2,)), dma((2,)), ring, ring,
                 dma, dma, dma, dma, dma, dma,
             ],
             compiler_params=pltpu.CompilerParams(

time: 73.7 us -> 72.4 us (0.982)
  Pallas kernels: 72.7 us -> 71.3 us
    pallas_call x1, Pallas kernels: 72.7 us -> 71.3 us  [shards(): pl.pallas_call(functools.partial(kernel, nx, ny, nc, nz), out_shape=pltpu...]
where the time goes in v4:
time: 72.4 us; the launch traced here: 72.2 us
  Pallas kernels  71.3 us (98%)
  local copies, waits for them, and re-layouts  0.83 us (1%)
    pallas_call x1, Pallas kernels, shards(): pl.pallas_call(functools.partial(kernel, nx, ny, nc, nz), out_shape=pltpu...  71.3 us

profile of v4, /device:TPU:1, one launch (start us, length us, event | category | flops | bytes accessed | tf_op | source)
XLA Modules:
  0.0 72.2 jit_solution(15994221415333514467)
XLA Ops:
  0.0 71.3 %shard_map.91 = bf16[624,512]{1,0:T(8,128)(2,1)S(1)} custom-call(bf16[208,1792]{1,0:T(8,128)(2,1)} %bitcast.7, bf16[208]{0:T(256)(128)(2,1)} %gain_hbm.1, bf16[208]{0:T(256)(128)(2,1)} %bias_hbm.1, bf16[832,1664]{1,0:T(8,128)(2,1)} %bitcast.6, bf16[208,512]{1,0:T(8,128)(2,1)} %bitcast.8, bf16[1664]{0:T(1024)(128)(2,1)} %norm_hbm.1, bf16[26,624]{1,0:T(8,128)(2,1)} %qkv_hbm.1, ...), custom_call_target="tpu_custom_call" | custom-call | tf_op jit(solution)/shard_map/pallas_call | solution.py:389
  71.3 0.8 %copy.11 = bf16[512,624]{0,1:T(8,128)(2,1)} copy(bf16[512,624]{0,1:T(8,128)(2,1)S(1)} %bitcast.5) | data formatting | bytes 1277952
